TPU v7x, 256 devices: a whole 4x4x8 slice. The times are simulated.
256 devices in a mesh: row: 8 (over z), col: 32 (over y, x, core).
Axes of the slice: x: 4, y: 4, z: 8, core: 2. Of those that a mesh axis runs over, the one named last changes fastest.
Arguments:
- factor_tiles: bfloat16 [3, 96, 64, 2048], P(None, 'row', None, 'col'), may hold values from -0.3125 to 0.3125
- tile_row: int32 [3, 96, 32], P(None, 'row', 'col'), may hold values from 0 to 63
- tile_col: int32 [3, 96, 32], P(None, 'row', 'col'), may hold values from 0 to 15
- right_sides: float32 [4, 512, 64, 128], P(None, ('col', 'row')), may hold values from -6 to 6
- diag_inverse: float32 [4, 64, 32768], P(None, None, ('col', 'row')), as said below
Outputs:
- preconditioned: float32 [4, 512, 64, 128], P(None, ('col', 'row'))
Inputs may be any that keep to these rules, and one draw needn't show every extreme that they name: `tile_row`: a block row within its row group. `tile_col`: a block column within its column group. `diag_inverse`: diagonal entries of every block between 0.5 and 2.
All inputs are finite; a program needn't handle non-finite values.
Results may differ from a plain program's by a relative error of at most 0.025.
Values may be sent and summed in bfloat16 or wider, within the bound.
A program may use at most 64 MiB of HBM per device.

v0:
```python
import jax
import jax.numpy as jnp
from jax import lax
from jax.sharding import PartitionSpec as P


def apply_inverse(inverse, vector, transposed):
    matrix = inverse.reshape(inverse.shape[0], -1, inverse.shape[0])
    if transposed:
        return jnp.einsum("cir,irn->icn", matrix, vector, precision=lax.Precision.HIGHEST)
    return jnp.einsum("cir,icn->irn", matrix, vector, precision=lax.Precision.HIGHEST)


def solve_all(factor_tiles, tile_row, tile_col, right_sides, diag_inverse):
    levels = factor_tiles.shape[0]
    rows_dev = right_sides.shape[1]
    group_rows = rows_dev * lax.axis_size("row")
    row_ids = tile_row[:, :, 0]
    col_ids = tile_col[:, :, 0]
    current = apply_inverse(diag_inverse[0], right_sides[0], False)
    solved = [current]
    for section_no in range(1, levels + 1):
        gathered = lax.all_gather(current.astype(jnp.bfloat16), "row", axis=0, tiled=True)
        picked = gathered[col_ids[section_no - 1]]
        products = jnp.einsum(
            "tab,tbn->tan", factor_tiles[section_no - 1], picked, preferred_element_type=jnp.float32
        )
        targets = row_ids[section_no - 1]

        def term(offset, length, products=products, targets=targets):
            places = jnp.arange(length, dtype=jnp.int32)
            select = (targets[:, None] == places[None, :]).astype(jnp.float32)
            return jnp.einsum("tq,tan->qan", select, products, precision=lax.Precision.HIGHEST)

        row_sums = lax.psum_scatter(
            term(jnp.int32(0), lax.axis_size("col") * rows_dev).astype(jnp.bfloat16),
            "col",
            scatter_dimension=0,
            tiled=True,
        ).astype(jnp.float32)
        current = apply_inverse(diag_inverse[section_no], right_sides[section_no] - row_sums, False)
        solved.append(current)
    current = apply_inverse(diag_inverse[levels], solved[levels], True)
    result = [current]
    columns_here = jnp.arange(group_rows, dtype=jnp.int32)
    for section_no in range(levels - 1, -1, -1):
        everyone = lax.all_gather(current.astype(jnp.bfloat16), "col", axis=0, tiled=True)
        picked = everyone[row_ids[section_no]]
        spread = jnp.einsum(
            "tab,tan->tbn", factor_tiles[section_no], picked, preferred_element_type=jnp.float32
        )
        select = (col_ids[section_no][:, None] == columns_here[None, :]).astype(jnp.float32)
        column_sums = jnp.einsum("tj,tbn->jbn", select, spread, precision=lax.Precision.HIGHEST)
        received = lax.psum_scatter(
            column_sums.astype(jnp.bfloat16), "row", scatter_dimension=0, tiled=True
        ).astype(jnp.float32)
        current = apply_inverse(diag_inverse[section_no], solved[section_no] - received, True)
        result.insert(0, current)
    return jnp.stack(result)


def on_device(factor_tiles, tile_row, tile_col, right_sides, diag_inverse):
    return solve_all(factor_tiles, tile_row, tile_col, right_sides, diag_inverse)


def solution(mesh):
    return jax.shard_map(
        on_device,
        mesh=mesh,
        in_specs=(
            P(None, "row", None, "col"),
            P(None, "row", "col"),
            P(None, "row", "col"),
            P(None, ("col", "row"), None, None),
            P(None, None, ("col", "row")),
        ),
        out_specs=P(None, ("col", "row"), None, None),
        check_vma=False,
    )
```

profile of v0, /device:TPU:2, one launch (start us, length us, event | category | flops | bytes accessed | tf_op | source)
XLA Modules:
  0.0 630.8 jit_solution(13500943562827002383)
XLA Ops:
  6.5 0.9 fusion.66
  7.4 0.1 copy.45
  7.5 1.0 fusion.67
  8.6 28.6 %all_gather.18 = bf16[16,64,128]{2,1,0:T(8,128)(2,1)S(1)} all-gather(bf16[2,64,128]{2,1,0:T(8,128)(2,1)S(1)} %get-tuple-element.21), channel_id=1, replica_groups=mesh['row'=8,'col'=32] {'row'}, dimensions={0}, use_global_device_ids=true | all-gather | bytes 294912 | tf_op jit(solution)/shard_map/all_gather | solution.py:23
  37.1 0.7 fusion.62
  37.8 0.7 slice_bitcast_fusion
  38.5 0.6 gather_fusion
  39.1 0.2 convolution_bitcast_fusion.2
  39.3 1.1 convolution_convert_fusion.2
  40.4 1.7 copy.47
  42.1 0.0 reduce-scatter.7.cloned.1.call-update
  42.1 0.0 reduce-scatter.9.cloned.1.call-start
  42.2 0.1 copy.48
  42.3 84.0 %reduce-scatter.7.cloned.1.call-done = bf16[2,64,128]{2,1,0:T(8,128)(2,1)} async-done(((bf16[64,64,128]{2,1,0:T(8,128)(2,1)}), bf16[2,64,128]{2,1,0:T(8,128)(2,1)}) %reduce-scatter.7.cloned.1.call-update) | async-done | bytes 32784 | tf_op jit(solution)/shard_map/reduce_scatter | solution.py:35
  126.3 1.0 fusion.68
  127.3 26.2 %all_gather.19 = bf16[16,64,128]{2,1,0:T(8,128)(2,1)S(1)} all-gather(bf16[2,64,128]{2,1,0:T(8,128)(2,1)S(1)} %get-tuple-element.23), channel_id=1, replica_groups=mesh['row'=8,'col'=32] {'row'}, dimensions={0}, use_global_device_ids=true | all-gather | bytes 294912 | tf_op jit(solution)/shard_map/all_gather | solution.py:23
  153.5 0.6 gather_fusion.1
  154.1 0.2 convolution_bitcast_fusion.1
  154.3 1.1 convolution_convert_fusion.1
  155.4 1.7 copy.50
  157.1 0.0 reduce-scatter.9.cloned.1.call-update
  157.1 0.0 reduce-scatter.11.cloned.1.call-start
  157.2 0.1 copy.51
  157.3 83.2 %reduce-scatter.9.cloned.1.call-done = bf16[2,64,128]{2,1,0:T(8,128)(2,1)} async-done(((bf16[64,64,128]{2,1,0:T(8,128)(2,1)}), bf16[2,64,128]{2,1,0:T(8,128)(2,1)}) %reduce-scatter.9.cloned.1.call-update) | async-done | bytes 32784 | tf_op jit(solution)/shard_map/reduce_scatter | solution.py:35
  240.5 1.0 fusion.69
  241.5 26.3 %all_gather.20 = bf16[16,64,128]{2,1,0:T(8,128)(2,1)S(1)} all-gather(bf16[2,64,128]{2,1,0:T(8,128)(2,1)S(1)} %get-tuple-element.25), channel_id=1, replica_groups=mesh['row'=8,'col'=32] {'row'}, dimensions={0}, use_global_device_ids=true | all-gather | bytes 294912 | tf_op jit(solution)/shard_map/all_gather | solution.py:23
  267.8 0.6 gather_fusion.2
  268.4 0.2 convolution_bitcast_fusion
  268.6 1.1 convolution_convert_fusion
  269.7 1.7 copy.53
  271.4 0.0 reduce-scatter.11.cloned.1.call-update
  271.4 0.0 all-gather.4.cloned.1.call-start
  271.4 0.1 reshape_squeeze.19
  271.5 83.2 %reduce-scatter.11.cloned.1.call-done = bf16[2,64,128]{2,1,0:T(8,128)(2,1)} async-done(((bf16[64,64,128]{2,1,0:T(8,128)(2,1)}), bf16[2,64,128]{2,1,0:T(8,128)(2,1)}) %reduce-scatter.11.cloned.1.call-update) | async-done | bytes 32784 | tf_op jit(solution)/shard_map/reduce_scatter | solution.py:35
  354.7 1.0 fusion.21
  355.7 0.8 bitcast_convert_fusion.2
  356.6 0.0 reduce-scatter.13.cloned.1.call-start
  356.7 48.0 %all-gather.4.cloned.1.call-done = bf16[64,64,128]{2,1,0:T(8,128)(2,1)} async-done(((bf16[2,64,128]{2,1,0:T(8,128)(2,1)}), bf16[64,64,128]{2,1,0:T(8,128)(2,1)}) %all-gather.4.cloned.1.call-update) | async-done | bytes 1048592 | tf_op jit(solution)/shard_map/all_gather | solution.py:47
  404.7 1.8 gather_fusion.3
  406.5 0.3 convolution_bitcast_fusion.5
  406.7 0.6 fusion.4
  407.3 0.8 copy.95
  408.1 0.0 reduce-scatter.13.cloned.1.call-update
  408.1 0.0 all-gather.6.cloned.1.call-start
  408.2 36.5 %reduce-scatter.13.cloned.1.call-done = bf16[2,64,128]{2,1,0:T(8,128)(2,1)} async-done(((bf16[16,64,128]{2,1,0:T(8,128)(2,1)}), bf16[2,64,128]{2,1,0:T(8,128)(2,1)}) %reduce-scatter.13.cloned.1.call-update) | async-done | bytes 32784 | tf_op jit(solution)/shard_map/reduce_scatter | solution.py:54
  444.7 1.7 bitcast_convert_fusion.1
  446.4 0.0 reduce-scatter.15.cloned.1.call-start
  446.4 46.9 %all-gather.6.cloned.1.call-done = bf16[64,64,128]{2,1,0:T(8,128)(2,1)} async-done(((bf16[2,64,128]{2,1,0:T(8,128)(2,1)}), bf16[64,64,128]{2,1,0:T(8,128)(2,1)}) %all-gather.6.cloned.1.call-update) | async-done | bytes 1048592 | tf_op jit(solution)/shard_map/all_gather | solution.py:47
  493.3 1.8 gather_fusion.4
  495.1 0.3 convolution_bitcast_fusion.4
  495.4 0.6 fusion.2
  496.0 0.8 copy.94
  496.8 0.0 all-gather.8.cloned.1.call-start
  496.8 36.5 %reduce-scatter.15.cloned.1.call-done = bf16[2,64,128]{2,1,0:T(8,128)(2,1)} async-done(((bf16[16,64,128]{2,1,0:T(8,128)(2,1)}), bf16[2,64,128]{2,1,0:T(8,128)(2,1)}) %reduce-scatter.15.cloned.1.call-update) | async-done | bytes 32784 | tf_op jit(solution)/shard_map/reduce_scatter | solution.py:54
  533.4 1.7 bitcast_convert_fusion
  535.0 0.0 reduce-scatter.17.cloned.1.call-start
  535.1 47.3 %all-gather.8.cloned.1.call-done = bf16[64,64,128]{2,1,0:T(8,128)(2,1)} async-done(((bf16[2,64,128]{2,1,0:T(8,128)(2,1)}), bf16[64,64,128]{2,1,0:T(8,128)(2,1)}) %all-gather.8.cloned.1.call-update) | async-done | bytes 1048592 | tf_op jit(solution)/shard_map/all_gather | solution.py:47
  582.4 1.8 gather_fusion.5
  584.2 0.3 convolution_bitcast_fusion.3
  584.5 0.6 fusion
  585.1 0.8 copy.93
  585.9 36.6 %reduce-scatter.17.cloned.1.call-done = bf16[2,64,128]{2,1,0:T(8,128)(2,1)} async-done(((bf16[16,64,128]{2,1,0:T(8,128)(2,1)}), bf16[2,64,128]{2,1,0:T(8,128)(2,1)}) %reduce-scatter.17.cloned.1.call-update) | async-done | bytes 32784 | tf_op jit(solution)/shard_map/reduce_scatter | solution.py:54
  622.5 1.0 convolution_bitcast_fusion.6
  623.5 0.7 pad_maximum_fusion
  (22 shorter events, 0.1 us)
Async XLA Ops:
  6.5 32.6 %copy-start = (bf16[3,12,64,64]{3,2,1,0:T(8,128)(2,1)S(1)}, bf16[3,12,64,64]{3,2,1,0:T(8,128)(2,1)}, u32[]{:S(2)}) copy-start(bf16[3,12,64,64]{3,2,1,0:T(8,128)(2,1)} %param.5) | copy-start | bytes 884740
  6.5 119.8 %reduce-scatter.7.cloned.1.call-start = ((), (), s32[]{:S(2)}) async-start(), calls=%async_computation.6 | async-start | bytes 1081344 | tf_op jit(solution)/shard_map/reduce_scatter | solution.py:35
  42.1 84.2 %copy-start.1 = (f32[4,2,64,128]{3,2,1,0:T(8,128)S(1)}, f32[4,2,64,128]{3,2,1,0:T(8,128)}, u32[]{:S(2)}) copy-start(f32[4,2,64,128]{3,2,1,0:T(8,128)} %param.8) | copy-start | bytes 786436
  42.1 198.4 %reduce-scatter.9.cloned.1.call-start = ((), (), s32[]{:S(2)}) async-start(), calls=%async_computation.7 | async-start | bytes 1081344 | tf_op jit(solution)/shard_map/reduce_scatter | solution.py:35
  157.1 197.6 %reduce-scatter.11.cloned.1.call-start = ((), (), s32[]{:S(2)}) async-start(), calls=%async_computation.8 | async-start | bytes 1081344 | tf_op jit(solution)/shard_map/reduce_scatter | solution.py:35
  271.4 85.3 %copy-start.2 = (s32[3,12,1]{1,2,0:T(1,128)S(1)}, s32[3,12,1]{1,2,0:T(1,128)}, u32[]{:S(2)}) copy-start(s32[3,12,1]{1,2,0:T(1,128)} %param.6) | copy-start | bytes 436
  271.4 85.3 %copy-start.3 = (s32[3,12,1]{1,2,0:T(1,128)S(1)}, s32[3,12,1]{1,2,0:T(1,128)}, u32[]{:S(2)}) copy-start(s32[3,12,1]{1,2,0:T(1,128)} %param.7) | copy-start | bytes 436
  271.4 133.3 %all-gather.4.cloned.1.call-start = ((), (), s32[]{:S(2)}) async-start(), calls=%async_computation.9 | async-start | bytes 1081344 | tf_op jit(solution)/shard_map/all_gather | solution.py:47
  356.6 88.1 %reduce-scatter.13.cloned.1.call-start = ((), (), s32[]{:S(2)}) async-start(), calls=%async_computation.10 | async-start | bytes 294912 | tf_op jit(solution)/shard_map/reduce_scatter | solution.py:54
  408.1 85.2 %all-gather.6.cloned.1.call-start = ((), (), s32[]{:S(2)}) async-start(), calls=%async_computation.11 | async-start | bytes 1081344 | tf_op jit(solution)/shard_map/all_gather | solution.py:47
  446.4 87.0 %reduce-scatter.15.cloned.1.call-start = ((), (), s32[]{:S(2)}) async-start(), calls=%async_computation.12 | async-start | bytes 294912 | tf_op jit(solution)/shard_map/reduce_scatter | solution.py:54
  496.8 85.7 %all-gather.8.cloned.1.call-start = ((), (), s32[]{:S(2)}) async-start(), calls=%async_computation.13 | async-start | bytes 1081344 | tf_op jit(solution)/shard_map/all_gather | solution.py:47
  535.0 87.4 %reduce-scatter.17.cloned.1.call-start = ((), (), s32[]{:S(2)}) async-start(), calls=%async_computation.14 | async-start | bytes 294912 | tf_op jit(solution)/shard_map/reduce_scatter | solution.py:54
Sparse Core Ops, SparseCore 0:
  42.2 84.0 reduce-scatter.6
  157.2 83.2 reduce-scatter.8
  271.5 83.1 reduce-scatter.10
  357.4 47.1 all-gather.3
  408.2 36.3 reduce-scatter.12
  447.1 46.1 all-gather.5
  496.9 36.4 reduce-scatter.14
  536.2 46.1 all-gather.7
  586.0 36.3 reduce-scatter.16
where the time goes:
time: 631 us
  waiting for transfers between devices  502 us (80%)
  blocking collectives  81.1 us (13%)
  local copies, waits for them, and re-layouts  16.5 us (3%)
  matrix products  15.6 us (2%)
  between operations  13.5 us (2%)
    reduce_scatter x3, waiting for transfers between devices, solve_all(): lax.psum_scatter(term(jnp.int32(0), lax.axis_size('col') * rows_dev).asty...  250 us
    all_gather x3, waiting for transfers between devices, solve_all(): lax.all_gather(current.astype(jnp.bfloat16), 'col', axis=0, tiled=True)  142 us
    reduce_scatter x3, waiting for transfers between devices, solve_all(): lax.psum_scatter(column_sums.astype(jnp.bfloat16), 'row', scatter_dimensi...  110 us
    all_gather x3, blocking collectives, solve_all(): lax.all_gather(current.astype(jnp.bfloat16), 'row', axis=0, tiled=True)  81.1 us
  transfers between devices with their start and end apart: 9, of which 9 were waited for; matrix products, arithmetic and copies ran while one was open for 0% of the time, Pallas kernels for 0%

commit v1 on v0

--- a/solution.py
+++ b/solution.py
@@ -2,6 +2,11 @@
 import jax.numpy as jnp
 from jax import lax
 from jax.sharding import PartitionSpec as P
+
+
+def gather_from_all(x, axis, dim):
+    copies = jnp.concatenate([x] * lax.axis_size(axis), axis=dim)
+    return lax.all_to_all(copies, axis, dim, dim, tiled=True)
 
 
 def apply_inverse(inverse, vector, transposed):
@@ -44,7 +49,7 @@
     result = [current]
     columns_here = jnp.arange(group_rows, dtype=jnp.int32)
     for section_no in range(levels - 1, -1, -1):
-        everyone = lax.all_gather(current.astype(jnp.bfloat16), "col", axis=0, tiled=True)
+        everyone = gather_from_all(current.astype(jnp.bfloat16), "col", 0)
         picked = everyone[row_ids[section_no]]
         spread = jnp.einsum(
             "tab,tan->tbn", factor_tiles[section_no], picked, preferred_element_type=jnp.float32

time: 631 us -> 603 us (0.956)
  waiting for transfers between devices: 502 us -> 400 us
  local copies, waits for them, and re-layouts: 16.5 us -> 69 us
  starting transfers between devices: 0.34 us -> 21 us
    all_gather x3 -> x0, waiting for transfers between devices: 142 us -> none  [solve_all(): lax.all_gather(current.astype(jnp.bfloat16), 'col', axis=0, tiled=True)]
    unnamed x8 -> x98, local copies, waits for them, and re-layouts: 0.01 us -> 54.4 us
    all_to_all x0 -> x3, waiting for transfers between devices: none -> 48.1 us  [gather_from_all(): return lax.all_to_all(copies, axis, dim, dim, tiled=True)]
    all_to_all x0 -> x3, starting transfers between devices: none -> 20.8 us  [gather_from_all(): return lax.all_to_all(copies, axis, dim, dim, tiled=True)]
    reduce_scatter x3, waiting for transfers between devices: 110 us -> 101 us  [solve_all(): lax.psum_scatter(column_sums.astype(jnp.bfloat16), 'row', scatter_dimensi...]
where the time goes in v1:
time: 603 us; the launch traced here: 602 us
  waiting for transfers between devices  400 us (66%)
  blocking collectives  81.1 us (13%)
  local copies, waits for them, and re-layouts  69 us (11%)
  starting transfers between devices  21 us (3%)
  matrix products  15.6 us (3%)
  between operations  13.8 us (2%)
    reduce_scatter x3, waiting for transfers between devices, solve_all(): lax.psum_scatter(term(jnp.int32(0), lax.axis_size('col') * rows_dev).asty...  250 us
    reduce_scatter x3, waiting for transfers between devices, solve_all(): lax.psum_scatter(column_sums.astype(jnp.bfloat16), 'row', scatter_dimensi...  101 us
    all_gather x3, blocking collectives, solve_all(): lax.all_gather(current.astype(jnp.bfloat16), 'row', axis=0, tiled=True)  81.1 us
    unnamed x98, local copies, waits for them, and re-layouts  54.4 us
    all_to_all x3, waiting for transfers between devices, gather_from_all(): return lax.all_to_all(copies, axis, dim, dim, tiled=True)  48.1 us
    all_to_all x3, starting transfers between devices, gather_from_all(): return lax.all_to_all(copies, axis, dim, dim, tiled=True)  20.8 us
  transfers between devices with their start and end apart: 9, of which 9 were waited for; matrix products, arithmetic and copies ran while one was open for 0% of the time, Pallas kernels for 0%

profile of v1, /device:TPU:2, one launch (start us, length us, event | category | flops | bytes accessed | tf_op | source)
XLA Modules:
  0.0 602.2 jit_solution(17335023149326834566)
XLA Ops:
  6.5 0.9 fusion.66
  7.5 1.0 fusion.67
  8.6 28.6 %all_gather.9 = bf16[16,64,128]{2,1,0:T(8,128)(2,1)S(1)} all-gather(bf16[2,64,128]{2,1,0:T(8,128)(2,1)S(1)} %get-tuple-element.27), channel_id=1, replica_groups=mesh['row'=8,'col'=32] {'row'}, dimensions={0}, use_global_device_ids=true | all-gather | bytes 294912 | tf_op jit(solution)/shard_map/all_gather | solution.py:28
  37.1 0.7 fusion.62
  37.8 0.7 slice_bitcast_fusion
  39.3 1.1 convolution_convert_fusion.2
  40.4 1.7 copy.47
  42.3 84.0 %reduce-scatter.7.cloned.1.call-done = bf16[2,64,128]{2,1,0:T(8,128)(2,1)} async-done(((bf16[64,64,128]{2,1,0:T(8,128)(2,1)}), bf16[2,64,128]{2,1,0:T(8,128)(2,1)}) %reduce-scatter.7.cloned.1.call-update) | async-done | bytes 32784 | tf_op jit(solution)/shard_map/reduce_scatter | solution.py:40
  126.3 1.0 fusion.68
  127.3 26.2 %all_gather.10 = bf16[16,64,128]{2,1,0:T(8,128)(2,1)S(1)} all-gather(bf16[2,64,128]{2,1,0:T(8,128)(2,1)S(1)} %get-tuple-element.29), channel_id=1, replica_groups=mesh['row'=8,'col'=32] {'row'}, dimensions={0}, use_global_device_ids=true | all-gather | bytes 294912 | tf_op jit(solution)/shard_map/all_gather | solution.py:28
  154.3 1.1 convolution_convert_fusion.1
  155.4 1.7 copy.50
  157.3 83.2 %reduce-scatter.9.cloned.1.call-done = bf16[2,64,128]{2,1,0:T(8,128)(2,1)} async-done(((bf16[64,64,128]{2,1,0:T(8,128)(2,1)}), bf16[2,64,128]{2,1,0:T(8,128)(2,1)}) %reduce-scatter.9.cloned.1.call-update) | async-done | bytes 32784 | tf_op jit(solution)/shard_map/reduce_scatter | solution.py:40
  240.5 1.0 fusion.69
  241.5 26.3 %all_gather.11 = bf16[16,64,128]{2,1,0:T(8,128)(2,1)S(1)} all-gather(bf16[2,64,128]{2,1,0:T(8,128)(2,1)S(1)} %get-tuple-element.31), channel_id=1, replica_groups=mesh['row'=8,'col'=32] {'row'}, dimensions={0}, use_global_device_ids=true | all-gather | bytes 294912 | tf_op jit(solution)/shard_map/all_gather | solution.py:28
  268.6 1.1 convolution_convert_fusion
  269.7 1.7 copy.53
  271.5 83.2 %reduce-scatter.11.cloned.1.call-done = bf16[2,64,128]{2,1,0:T(8,128)(2,1)} async-done(((bf16[64,64,128]{2,1,0:T(8,128)(2,1)}), bf16[2,64,128]{2,1,0:T(8,128)(2,1)}) %reduce-scatter.11.cloned.1.call-update) | async-done | bytes 32784 | tf_op jit(solution)/shard_map/reduce_scatter | solution.py:40
  354.7 1.0 fusion.21
  355.8 0.8 constant_dynamic-update-slice_fusion.31
  359.6 0.6 constant_dynamic-update-slice_fusion.25
  360.8 0.6 constant_dynamic-update-slice_fusion.23
  362.0 0.6 constant_dynamic-update-slice_fusion.21
  367.4 0.6 constant_dynamic-update-slice_fusion.12
  368.1 0.6 constant_dynamic-update-slice_fusion.11
  369.3 0.6 constant_dynamic-update-slice_fusion.9
  369.9 0.6 constant_dynamic-update-slice_fusion.8
  370.5 0.6 constant_dynamic-update-slice_fusion.7
  371.7 0.6 constant_dynamic-update-slice_fusion.5
  372.9 0.6 constant_dynamic-update-slice_fusion.3
  375.3 6.0 all-to-all-start
  381.4 16.0 %all-to-all-done = bf16[64,64,128]{2,1,0:T(8,128)(2,1)S(1)} async-done(((bf16[64,64,128]{2,1,0:T(8,128)(2,1)}), bf16[64,64,128]{2,1,0:T(8,128)(2,1)S(1)}, u32[]{:S(2)}, u32[]{:S(2)}) %all-to-all-start) | async-done | bytes 1048608 | tf_op jit(solution)/shard_map/all_to_all | solution.py:9
  398.9 0.8 copy.95
  399.7 35.6 %reduce-scatter.13.cloned.1.call-done = bf16[2,64,128]{2,1,0:T(8,128)(2,1)} async-done(((bf16[16,64,128]{2,1,0:T(8,128)(2,1)}), bf16[2,64,128]{2,1,0:T(8,128)(2,1)}) %reduce-scatter.13.cloned.1.call-update) | async-done | bytes 32784 | tf_op jit(solution)/shard_map/reduce_scatter | solution.py:59
  435.2 1.7 constant_dynamic-update-slice_fusion.63
  439.9 0.6 constant_dynamic-update-slice_fusion.57
  441.1 0.6 constant_dynamic-update-slice_fusion.55
  442.3 0.6 constant_dynamic-update-slice_fusion.53
  447.8 0.6 constant_dynamic-update-slice_fusion.44
  449.6 0.6 constant_dynamic-update-slice_fusion.41
  450.2 0.6 constant_dynamic-update-slice_fusion.40
  450.8 0.6 constant_dynamic-update-slice_fusion.39
  452.0 0.6 constant_dynamic-update-slice_fusion.37
  453.2 0.6 constant_dynamic-update-slice_fusion.35
  455.7 7.4 %all-to-all-start.1 = ((bf16[64,64,128]{2,1,0:T(8,128)(2,1)}), bf16[64,64,128]{2,1,0:T(8,128)(2,1)S(1)}, u32[]{:S(2)}, u32[]{:S(2)}) async-start(bf16[64,64,128]{2,1,0:T(8,128)(2,1)} %constant_dynamic-update-slice_fusion.32), calls=%async_computation.5 | async-start | bytes 2097152 | tf_op jit(solution)/shard_map/all_to_all | solution.py:9
  463.1 16.1 %all-to-all-done.1 = bf16[64,64,128]{2,1,0:T(8,128)(2,1)S(1)} async-done(((bf16[64,64,128]{2,1,0:T(8,128)(2,1)}), bf16[64,64,128]{2,1,0:T(8,128)(2,1)S(1)}, u32[]{:S(2)}, u32[]{:S(2)}) %all-to-all-start.1) | async-done | bytes 1048608 | tf_op jit(solution)/shard_map/all_to_all | solution.py:9
  480.6 0.8 copy.94
  481.4 32.9 %reduce-scatter.15.cloned.1.call-done = bf16[2,64,128]{2,1,0:T(8,128)(2,1)} async-done(((bf16[16,64,128]{2,1,0:T(8,128)(2,1)}), bf16[2,64,128]{2,1,0:T(8,128)(2,1)}) %reduce-scatter.15.cloned.1.call-update) | async-done | bytes 32784 | tf_op jit(solution)/shard_map/reduce_scatter | solution.py:59
  514.4 1.7 constant_dynamic-update-slice_fusion.95
  519.1 0.6 constant_dynamic-update-slice_fusion.89
  520.3 0.6 constant_dynamic-update-slice_fusion.87
  521.5 0.6 constant_dynamic-update-slice_fusion.85
  526.9 0.6 constant_dynamic-update-slice_fusion.76
  528.7 0.6 constant_dynamic-update-slice_fusion.73
  529.4 0.6 constant_dynamic-update-slice_fusion.72
  530.0 0.6 constant_dynamic-update-slice_fusion.71
  531.2 0.6 constant_dynamic-update-slice_fusion.69
  532.4 0.6 constant_dynamic-update-slice_fusion.67
  534.8 7.4 %all-to-all-start.2 = ((bf16[64,64,128]{2,1,0:T(8,128)(2,1)}), bf16[64,64,128]{2,1,0:T(8,128)(2,1)S(1)}, u32[]{:S(2)}, u32[]{:S(2)}) async-start(bf16[64,64,128]{2,1,0:T(8,128)(2,1)} %constant_dynamic-update-slice_fusion.64), calls=%async_computation.7 | async-start | bytes 2097152 | tf_op jit(solution)/shard_map/all_to_all | solution.py:9
  542.3 16.1 %all-to-all-done.2 = bf16[64,64,128]{2,1,0:T(8,128)(2,1)S(1)} async-done(((bf16[64,64,128]{2,1,0:T(8,128)(2,1)}), bf16[64,64,128]{2,1,0:T(8,128)(2,1)S(1)}, u32[]{:S(2)}, u32[]{:S(2)}) %all-to-all-start.2) | async-done | bytes 1048608 | tf_op jit(solution)/shard_map/all_to_all | solution.py:9
  559.8 0.8 copy.93
  560.6 33.0 %reduce-scatter.17.cloned.1.call-done = bf16[2,64,128]{2,1,0:T(8,128)(2,1)} async-done(((bf16[16,64,128]{2,1,0:T(8,128)(2,1)}), bf16[2,64,128]{2,1,0:T(8,128)(2,1)}) %reduce-scatter.17.cloned.1.call-update) | async-done | bytes 32784 | tf_op jit(solution)/shard_map/reduce_scatter | solution.py:59
  593.5 1.0 convolution_bitcast_fusion.6
  594.6 0.7 pad_maximum_fusion
  (112 shorter events, 46.5 us)
Async XLA Ops:
  6.5 32.6 %copy-start = (bf16[3,12,64,64]{3,2,1,0:T(8,128)(2,1)S(1)}, bf16[3,12,64,64]{3,2,1,0:T(8,128)(2,1)}, u32[]{:S(2)}) copy-start(bf16[3,12,64,64]{3,2,1,0:T(8,128)(2,1)} %param.5) | copy-start | bytes 884740
  6.5 119.8 %reduce-scatter.7.cloned.1.call-start = ((), (), s32[]{:S(2)}) async-start(), calls=%async_computation.9 | async-start | bytes 1081344 | tf_op jit(solution)/shard_map/reduce_scatter | solution.py:40
  42.1 84.2 %copy-start.1 = (f32[4,2,64,128]{3,2,1,0:T(8,128)S(1)}, f32[4,2,64,128]{3,2,1,0:T(8,128)}, u32[]{:S(2)}) copy-start(f32[4,2,64,128]{3,2,1,0:T(8,128)} %param.8) | copy-start | bytes 786436
  42.1 198.4 %reduce-scatter.9.cloned.1.call-start = ((), (), s32[]{:S(2)}) async-start(), calls=%async_computation.10 | async-start | bytes 1081344 | tf_op jit(solution)/shard_map/reduce_scatter | solution.py:40
  157.1 197.6 %reduce-scatter.11.cloned.1.call-start = ((), (), s32[]{:S(2)}) async-start(), calls=%async_computation.11 | async-start | bytes 1081344 | tf_op jit(solution)/shard_map/reduce_scatter | solution.py:40
  375.3 6.0 %copy-start.2 = (s32[3,12,1]{1,2,0:T(1,128)S(1)}, s32[3,12,1]{1,2,0:T(1,128)}, u32[]{:S(2)}) copy-start(s32[3,12,1]{1,2,0:T(1,128)} %param.6) | copy-start | bytes 436
  375.3 6.1 %copy-start.3 = (s32[3,12,1]{1,2,0:T(1,128)S(1)}, s32[3,12,1]{1,2,0:T(1,128)}, u32[]{:S(2)}) copy-start(s32[3,12,1]{1,2,0:T(1,128)} %param.7) | copy-start | bytes 436
  375.3 22.1 %all-to-all-start = ((bf16[64,64,128]{2,1,0:T(8,128)(2,1)}), bf16[64,64,128]{2,1,0:T(8,128)(2,1)S(1)}, u32[]{:S(2)}, u32[]{:S(2)}) async-start(bf16[64,64,128]{2,1,0:T(8,128)(2,1)} %constant_dynamic-update-slice_fusion), calls=%async_computation.3 | async-start | bytes 2097152 | tf_op jit(solution)/shard_map/all_to_all | solution.py:9
  381.3 53.9 %reduce-scatter.13.cloned.1.call-start = ((), (), s32[]{:S(2)}) async-start(), calls=%async_computation.12 | async-start | bytes 294912 | tf_op jit(solution)/shard_map/reduce_scatter | solution.py:59
  455.7 23.5 %all-to-all-start.1 = ((bf16[64,64,128]{2,1,0:T(8,128)(2,1)}), bf16[64,64,128]{2,1,0:T(8,128)(2,1)S(1)}, u32[]{:S(2)}, u32[]{:S(2)}) async-start(bf16[64,64,128]{2,1,0:T(8,128)(2,1)} %constant_dynamic-update-slice_fusion.32), calls=%async_computation.5 | async-start | bytes 2097152 | tf_op jit(solution)/shard_map/all_to_all | solution.py:9
  463.1 51.3 %reduce-scatter.15.cloned.1.call-start = ((), (), s32[]{:S(2)}) async-start(), calls=%async_computation.13 | async-start | bytes 294912 | tf_op jit(solution)/shard_map/reduce_scatter | solution.py:59
  534.8 23.5 %all-to-all-start.2 = ((bf16[64,64,128]{2,1,0:T(8,128)(2,1)}), bf16[64,64,128]{2,1,0:T(8,128)(2,1)S(1)}, u32[]{:S(2)}, u32[]{:S(2)}) async-start(bf16[64,64,128]{2,1,0:T(8,128)(2,1)} %constant_dynamic-update-slice_fusion.64), calls=%async_computation.7 | async-start | bytes 2097152 | tf_op jit(solution)/shard_map/all_to_all | solution.py:9
  542.2 51.3 %reduce-scatter.17.cloned.1.call-start = ((), (), s32[]{:S(2)}) async-start(), calls=%async_computation.14 | async-start | bytes 294912 | tf_op jit(solution)/shard_map/reduce_scatter | solution.py:59
Sparse Core Ops, SparseCore 0:
  42.2 84.0 reduce-scatter.6
  157.2 83.2 reduce-scatter.8
  271.5 83.1 reduce-scatter.10
  399.8 35.3 reduce-scatter.12
  481.6 32.7 reduce-scatter.14
  560.7 32.7 reduce-scatter.16
